TPU v7x, 32 devices: a whole 2x2x4 slice. The times are simulated.
32 devices in a mesh: ind: 4 (over x, core), mark: 4 (over z), chip: 2 (over y).
Axes of the slice: x: 2, y: 2, z: 4, core: 2. Of those that a mesh axis runs over, the one named last changes fastest.
Arguments:
- genotypes: bfloat16 [8192, 8192], P(('ind', 'chip'), 'mark'), may hold values from -0.1875 to 0.1875
- residual: float32 [8192, 1024], P(('ind', 'chip'), 'mark'), as said below
- posterior_inverse: bfloat16 [8, 1024, 1024], P('mark'), as said below
- gibbs_noise: bfloat16 [4, 8192, 256], P(None, 'mark'), may hold values from -6 to 6
- visit_order: int32 [4, 4, 2], P(None, 'mark'), may hold values from 0 to 1, each once within a row
Outputs:
- residual_after: float32 [8192, 1024], P(('ind', 'chip'), 'mark')
- effect_changes: float32 [4, 8192, 256], P(None, 'mark')
Inputs may be any that keep to these rules, and one draw needn't show every extreme that they name: `visit_order`: each row names each of the 2 marker blocks of one cycle position once. `residual`: finite real values. `posterior_inverse`: the diagonal entries are positive.
All inputs are finite; a program needn't handle non-finite values.
Results may differ from a plain program's by a relative error of at most 0.005.
Values sent between devices are 32-bit elements; how exact they have to be, the bound alone decides.
A program may use at most 128 MiB of HBM per device.

v0:
```python
import jax
import jax.numpy as jnp
from jax import lax
from jax.sharding import PartitionSpec as P

epsilon = 1e-05


def from_behind(array, axis, by):
    peers = lax.axis_size(axis)
    return lax.ppermute(array, axis, [(i, (i + by) % peers) for i in range(peers)])


def posterior_step(inverse, scores, total_sq, noise_rows, count):
    spread = total_sq / count
    scaled = (scores / count).astype(jnp.bfloat16)
    mean_part = jnp.dot(inverse, scaled, preferred_element_type=jnp.float32)
    diag_part = jnp.diagonal(inverse).astype(jnp.float32)
    return (
        mean_part + jnp.sqrt(diag_part[:, None] * (spread[None, :] + epsilon) / count) * noise_rows
    )


def local(genotypes, residual, posterior_inverse, gibbs_noise, visit_order):
    cycle_size = lax.axis_size("mark")
    groups = lax.axis_size("ind") * lax.axis_size("chip")
    count = genotypes.shape[0] * groups
    width = residual.shape[1]
    block_len = posterior_inverse.shape[1]
    blocks_here = posterior_inverse.shape[0]
    current = residual
    change_list = []
    for stop_idx in range(cycle_size):
        stop_changes = jnp.zeros((blocks_here * block_len, width), jnp.float32)
        for visit_pos in range(blocks_here):
            local_blk = visit_order[stop_idx, 0, visit_pos]
            columns = lax.dynamic_slice_in_dim(genotypes, local_blk * block_len, block_len, 1)
            sq_part = jnp.sum(current * current, axis=0)
            inverse = lax.dynamic_index_in_dim(posterior_inverse, local_blk, 0, keepdims=False)
            noise_rows = lax.slice_in_dim(
                gibbs_noise[stop_idx], visit_pos * block_len, (visit_pos + 1) * block_len, axis=0
            ).astype(jnp.float32)
            current_low = current.astype(jnp.bfloat16)
            partial_value = lax.dot_general(
                columns, current_low, (((0,), (0,)), ((), ())), preferred_element_type=jnp.float32
            )
            scores, total_sq = lax.psum((partial_value, sq_part), ("ind", "chip"))
            change = posterior_step(inverse, scores, total_sq, noise_rows, count)
            stop_changes = lax.dynamic_update_slice_in_dim(
                stop_changes, change, local_blk * block_len, 0
            )
            current = current - jnp.dot(
                columns, change.astype(jnp.bfloat16), preferred_element_type=jnp.float32
            )
        change_list.append(stop_changes)
        current = from_behind(current, "mark", 1)
    return (current, jnp.stack(change_list))


def solution(mesh):
    in_specs = (
        P(("ind", "chip"), "mark"),
        P(("ind", "chip"), "mark"),
        P("mark", None, None),
        P(None, "mark", None),
        P(None, "mark", None),
    )
    out_specs = (P(("ind", "chip"), "mark"), P(None, "mark", None))
    return jax.shard_map(local, mesh=mesh, in_specs=in_specs, out_specs=out_specs, check_vma=False)
```

profile of v0, /device:TPU:0, one launch (start us, length us, event | category | flops | bytes accessed | tf_op | source)
XLA Modules:
  0.0 635.7 jit_solution(9045469736230866958)
XLA Ops:
  9.5 3.6 fusion.30
  27.6 11.6 %dynamic-slice_bitcast_fusion = (bf16[1024,1024]{1,0:T(8,128)(2,1)S(1)}, bf16[1024,1024]{1,0:T(8,128)(2,1)}, bf16[1024,1024]{1,0:T(8,128)(2,1)}, bf16[1024,1024]...) fusion(bf16[2,1024,1024]{2,1,0:T(8,128)(2,1)} %param.7, ...), kind=kLoop, calls=%fused_computation.9 | loop fusion | bytes 33554464 | tf_op jit(solution)/shard_map/jit(dynamic_index_in_dim)/squeeze | solution.py:39
  40.0 16.4 %gather_fusion = bf16[1024]{0:T(1024)(128)(2,1)S(1)} fusion(bf16[1024,1024]{1,0:T(8,128)(2,1)} %get-tuple-element.8, s32[1024]{0:T(1024)S(1)} %bitcast.81), kind=kCustom, calls=%fused_computation | custom fusion | bytes 12288 | tf_op jit(solution)/shard_map/jit(diagonal)/cond/branch_0_fun/gather | solution.py:18
  56.6 15.3 %psum.113 = f32[256]{0:T(256)S(1)} all-reduce(f32[256]{0:T(256)S(1)} %multiply_reduce_fusion.7), channel_id=1, replica_groups=mesh['ind'=4,'mark'=4,'chip'=2] {'ind','chip'}, use_global_device_ids=true, to_apply=%region_2.3 | all-reduce | flops 256 | bytes 2048 | tf_op jit(solution)/shard_map/psum | solution.py:47
  74.3 2.6 bitcast_dynamic-update-slice_fusion.7
  78.2 1.8 fusion.26
  80.0 16.0 %gather_fusion.1 = bf16[1024]{0:T(1024)(128)(2,1)S(1)} fusion(bf16[1024,1024]{1,0:T(8,128)(2,1)} %get-tuple-element.7, s32[1024]{0:T(1024)S(1)} %bitcast.82), kind=kCustom, calls=%fused_computation.1 | custom fusion | bytes 12288 | tf_op jit(solution)/shard_map/jit(diagonal)/cond/branch_0_fun/gather | solution.py:18
  96.0 12.5 %psum.115 = f32[256]{0:T(256)S(1)} all-reduce(f32[256]{0:T(256)S(1)} %get-tuple-element.18), channel_id=1, replica_groups=mesh['ind'=4,'mark'=4,'chip'=2] {'ind','chip'}, use_global_device_ids=true, to_apply=%region_5.6 | all-reduce | flops 256 | bytes 2048 | tf_op jit(solution)/shard_map/psum | solution.py:47
  108.5 28.1 %all-reduce.11.cloned.1.call-done = f32[1024,256]{1,0:T(8,128)} async-done(((f32[1024,256]{1,0:T(8,128)}), f32[1024,256]{1,0:T(8,128)}) %all-reduce.11.cloned.1.call-update) | async-done | bytes 1048592 | tf_op jit(solution)/shard_map/psum | solution.py:47
  136.6 4.1 bitcast_dynamic-update-slice_fusion.6
  140.7 1.7 fusion.35
  144.6 23.9 %collective-permute-done = f32[1024,256]{1,0:T(8,128)S(1)} collective-permute-done((f32[1024,256]{1,0:T(8,128)}, f32[1024,256]{1,0:T(8,128)S(1)}, u32[]{:S(2)}, u32[]{:S(2)}) %collective-permute-start) | collective-permute-done | bytes 1048608 | tf_op jit(solution)/shard_map/ppermute | solution.py:11
  168.5 3.7 fusion.22
  172.8 16.1 %gather_fusion.2 = bf16[1024]{0:T(1024)(128)(2,1)S(1)} fusion(bf16[1024,1024]{1,0:T(8,128)(2,1)} %get-tuple-element.6, s32[1024]{0:T(1024)S(1)} %bitcast.83), kind=kCustom, calls=%fused_computation.2 | custom fusion | bytes 12288 | tf_op jit(solution)/shard_map/jit(diagonal)/cond/branch_0_fun/gather | solution.py:18
  189.1 12.6 %psum.117 = f32[256]{0:T(256)S(1)} all-reduce(f32[256]{0:T(256)S(1)} %multiply_reduce_fusion.5), channel_id=1, replica_groups=mesh['ind'=4,'mark'=4,'chip'=2] {'ind','chip'}, use_global_device_ids=true, to_apply=%region_8.9 | all-reduce | flops 256 | bytes 2048 | tf_op jit(solution)/shard_map/psum | solution.py:47
  201.7 25.2 %all-reduce.13.cloned.1.call-done = f32[1024,256]{1,0:T(8,128)} async-done(((f32[1024,256]{1,0:T(8,128)}), f32[1024,256]{1,0:T(8,128)}) %all-reduce.13.cloned.1.call-update) | async-done | bytes 1048592 | tf_op jit(solution)/shard_map/psum | solution.py:47
  228.5 2.6 bitcast_dynamic-update-slice_fusion.5
  232.4 1.8 fusion.18
  234.2 16.2 %gather_fusion.3 = bf16[1024]{0:T(1024)(128)(2,1)S(1)} fusion(bf16[1024,1024]{1,0:T(8,128)(2,1)} %get-tuple-element.5, s32[1024]{0:T(1024)S(1)} %bitcast.84), kind=kCustom, calls=%fused_computation.3 | custom fusion | bytes 12288 | tf_op jit(solution)/shard_map/jit(diagonal)/cond/branch_0_fun/gather | solution.py:18
  250.4 12.5 %psum.119 = f32[256]{0:T(256)S(1)} all-reduce(f32[256]{0:T(256)S(1)} %get-tuple-element.20), channel_id=1, replica_groups=mesh['ind'=4,'mark'=4,'chip'=2] {'ind','chip'}, use_global_device_ids=true, to_apply=%region_11.12 | all-reduce | flops 256 | bytes 2048 | tf_op jit(solution)/shard_map/psum | solution.py:47
  262.9 27.4 %all-reduce.15.cloned.1.call-done = f32[1024,256]{1,0:T(8,128)} async-done(((f32[1024,256]{1,0:T(8,128)}), f32[1024,256]{1,0:T(8,128)}) %all-reduce.15.cloned.1.call-update) | async-done | bytes 1048592 | tf_op jit(solution)/shard_map/psum | solution.py:47
  290.3 4.2 bitcast_dynamic-update-slice_fusion.4
  294.5 1.7 fusion.41
  298.2 24.0 %collective-permute-done.1 = f32[1024,256]{1,0:T(8,128)S(1)} collective-permute-done((f32[1024,256]{1,0:T(8,128)}, f32[1024,256]{1,0:T(8,128)S(1)}, u32[]{:S(2)}, u32[]{:S(2)}) %collective-permute-start.1) | collective-permute-done | bytes 1048608 | tf_op jit(solution)/shard_map/ppermute | solution.py:11
  322.2 3.8 fusion.14
  326.6 16.2 %gather_fusion.4 = bf16[1024]{0:T(1024)(128)(2,1)S(1)} fusion(bf16[1024,1024]{1,0:T(8,128)(2,1)} %get-tuple-element.4, s32[1024]{0:T(1024)S(1)} %bitcast.85), kind=kCustom, calls=%fused_computation.4 | custom fusion | bytes 12288 | tf_op jit(solution)/shard_map/jit(diagonal)/cond/branch_0_fun/gather | solution.py:18
  343.0 12.4 %psum.121 = f32[256]{0:T(256)S(1)} all-reduce(f32[256]{0:T(256)S(1)} %multiply_reduce_fusion.3), channel_id=1, replica_groups=mesh['ind'=4,'mark'=4,'chip'=2] {'ind','chip'}, use_global_device_ids=true, to_apply=%region_14.15 | all-reduce | flops 256 | bytes 2048 | tf_op jit(solution)/shard_map/psum | solution.py:47
  355.4 25.2 %all-reduce.17.cloned.1.call-done = f32[1024,256]{1,0:T(8,128)} async-done(((f32[1024,256]{1,0:T(8,128)}), f32[1024,256]{1,0:T(8,128)}) %all-reduce.17.cloned.1.call-update) | async-done | bytes 1048592 | tf_op jit(solution)/shard_map/psum | solution.py:47
  382.2 2.6 bitcast_dynamic-update-slice_fusion.3
  386.2 1.8 fusion.10
  388.0 15.8 %gather_fusion.5 = bf16[1024]{0:T(1024)(128)(2,1)S(1)} fusion(bf16[1024,1024]{1,0:T(8,128)(2,1)} %get-tuple-element.3, s32[1024]{0:T(1024)S(1)} %bitcast.86), kind=kCustom, calls=%fused_computation.5 | custom fusion | bytes 12288 | tf_op jit(solution)/shard_map/jit(diagonal)/cond/branch_0_fun/gather | solution.py:18
  403.9 12.5 %psum.123 = f32[256]{0:T(256)S(1)} all-reduce(f32[256]{0:T(256)S(1)} %get-tuple-element.22), channel_id=1, replica_groups=mesh['ind'=4,'mark'=4,'chip'=2] {'ind','chip'}, use_global_device_ids=true, to_apply=%region_17.18 | all-reduce | flops 256 | bytes 2048 | tf_op jit(solution)/shard_map/psum | solution.py:47
  416.4 27.7 %all-reduce.19.cloned.1.call-done = f32[1024,256]{1,0:T(8,128)} async-done(((f32[1024,256]{1,0:T(8,128)}), f32[1024,256]{1,0:T(8,128)}) %all-reduce.19.cloned.1.call-update) | async-done | bytes 1048592 | tf_op jit(solution)/shard_map/psum | solution.py:47
  444.1 4.2 bitcast_dynamic-update-slice_fusion.2
  448.3 1.7 fusion.47
  452.0 24.0 %collective-permute-done.2 = f32[1024,256]{1,0:T(8,128)S(1)} collective-permute-done((f32[1024,256]{1,0:T(8,128)}, f32[1024,256]{1,0:T(8,128)S(1)}, u32[]{:S(2)}, u32[]{:S(2)}) %collective-permute-start.2) | collective-permute-done | bytes 1048608 | tf_op jit(solution)/shard_map/ppermute | solution.py:11
  476.1 3.7 fusion.6
  480.4 16.0 %gather_fusion.6 = bf16[1024]{0:T(1024)(128)(2,1)S(1)} fusion(bf16[1024,1024]{1,0:T(8,128)(2,1)} %get-tuple-element.9, s32[1024]{0:T(1024)S(1)} %bitcast.87), kind=kCustom, calls=%fused_computation.6 | custom fusion | bytes 12288 | tf_op jit(solution)/shard_map/jit(diagonal)/cond/branch_0_fun/gather | solution.py:18
  496.6 12.4 %psum.125 = f32[256]{0:T(256)S(1)} all-reduce(f32[256]{0:T(256)S(1)} %multiply_reduce_fusion.1), channel_id=1, replica_groups=mesh['ind'=4,'mark'=4,'chip'=2] {'ind','chip'}, use_global_device_ids=true, to_apply=%region_20.21 | all-reduce | flops 256 | bytes 2048 | tf_op jit(solution)/shard_map/psum | solution.py:47
  509.0 25.4 %all-reduce.21.cloned.1.call-done = f32[1024,256]{1,0:T(8,128)} async-done(((f32[1024,256]{1,0:T(8,128)}), f32[1024,256]{1,0:T(8,128)}) %all-reduce.21.cloned.1.call-update) | async-done | bytes 1048592 | tf_op jit(solution)/shard_map/psum | solution.py:47
  536.0 2.6 bitcast_dynamic-update-slice_fusion.1
  539.9 1.8 fusion.2
  541.7 9.2 %gather_fusion.7 = bf16[1024]{0:T(1024)(128)(2,1)S(1)} fusion(bf16[1024,1024]{1,0:T(8,128)(2,1)S(1)} %get-tuple-element.2, s32[1024]{0:T(1024)S(1)} %bitcast.88), kind=kCustom, calls=%fused_computation.7 | custom fusion | bytes 12288 | tf_op jit(solution)/shard_map/jit(diagonal)/cond/branch_0_fun/gather | solution.py:18
  550.9 12.5 %psum.127 = f32[256]{0:T(256)S(1)} all-reduce(f32[256]{0:T(256)S(1)} %get-tuple-element.24), channel_id=1, replica_groups=mesh['ind'=4,'mark'=4,'chip'=2] {'ind','chip'}, use_global_device_ids=true, to_apply=%region_23.24 | all-reduce | flops 256 | bytes 2048 | tf_op jit(solution)/shard_map/psum | solution.py:47
  563.3 34.4 %all-reduce.23.cloned.1.call-done = f32[1024,256]{1,0:T(8,128)} async-done(((f32[1024,256]{1,0:T(8,128)}), f32[1024,256]{1,0:T(8,128)}) %all-reduce.23.cloned.1.call-update) | async-done | bytes 1048592 | tf_op jit(solution)/shard_map/psum | solution.py:47
  597.8 3.5 bitcast_dynamic-update-slice_fusion
  603.5 5.3 pad_maximum_fusion
  608.8 19.1 %collective-permute-done.3 = f32[1024,256]{1,0:T(8,128)S(1)} collective-permute-done((f32[1024,256]{1,0:T(8,128)S(1)}, f32[1024,256]{1,0:T(8,128)S(1)}, u32[]{:S(2)}, u32[]{:S(2)}) %collective-permute-start.3) | collective-permute-done | bytes 1048608 | tf_op jit(solution)/shard_map/ppermute | solution.py:11
  (105 shorter events, 22.8 us)
Async XLA Ops:
  7.2 65.5 %all-reduce.9.cloned.1.call-start = ((), (), s32[]{:S(2)}) async-start(), calls=%async_computation | async-start | bytes 2097152 | tf_op jit(solution)/shard_map/psum | solution.py:47
  13.1 123.5 %all-reduce.11.cloned.1.call-start = ((), (), s32[]{:S(2)}) async-start(), calls=%async_computation.1 | async-start | bytes 2097152 | tf_op jit(solution)/shard_map/psum | solution.py:47
  39.3 17.2 %copy-start.18 = (f32[1024,256]{1,0:T(8,128)S(1)}, f32[1024,256]{1,0:T(8,128)}, u32[]{:S(2)}) copy-start(f32[1024,256]{1,0:T(8,128)} %param.6) | copy-start | bytes 3145732
  72.7 1.6 copy-start.11
  74.3 2.7 copy-start
  74.3 3.0 copy-start.19
  76.9 1.3 copy-start.14
  80.0 146.9 %all-reduce.13.cloned.1.call-start = ((), (), s32[]{:S(2)}) async-start(), calls=%async_computation.2 | async-start | bytes 2097152 | tf_op jit(solution)/shard_map/psum | solution.py:47
  136.6 4.1 copy-start.1
  142.4 26.0 %collective-permute-start = (f32[1024,256]{1,0:T(8,128)}, f32[1024,256]{1,0:T(8,128)S(1)}, u32[]{:S(2)}, u32[]{:S(2)}) collective-permute-start(f32[1024,256]{1,0:T(8,128)} %fusion.35), channel_id=1, source_target_pairs={{0,2},{2,4},{4,6},{6,0},{1,3},{3,5},{5,7},{7,1},{8,10},{10,12},{12... | collective-permute-start | bytes 3145736 | tf_op jit(solution)/shard_map/ppermute | solution.py:11
  168.5 20.4 %copy-start.22 = (f32[1024,256]{1,0:T(8,128)}, f32[1024,256]{1,0:T(8,128)S(1)}, u32[]{:S(2)}) copy-start(f32[1024,256]{1,0:T(8,128)S(1)} %collective-permute-done) | copy-start | bytes 3145732
  172.2 118.1 %all-reduce.15.cloned.1.call-start = ((), (), s32[]{:S(2)}) async-start(), calls=%async_computation.3 | async-start | bytes 2097152 | tf_op jit(solution)/shard_map/psum | solution.py:47
  226.9 1.6 copy-start.10
  228.5 2.7 copy-start.2
  228.5 3.0 copy-start.23
  231.0 1.3 copy-start.16
  234.2 146.5 %all-reduce.17.cloned.1.call-start = ((), (), s32[]{:S(2)}) async-start(), calls=%async_computation.4 | async-start | bytes 2097152 | tf_op jit(solution)/shard_map/psum | solution.py:47
  290.3 4.2 copy-start.3
  296.2 26.0 %collective-permute-start.1 = (f32[1024,256]{1,0:T(8,128)}, f32[1024,256]{1,0:T(8,128)S(1)}, u32[]{:S(2)}, u32[]{:S(2)}) collective-permute-start(f32[1024,256]{1,0:T(8,128)} %fusion.41), channel_id=1, source_target_pairs={{0,2},{2,4},{4,6},{6,0},{1,3},{3,5},{5,7},{7,1},{8,10},{10,12},{12... | collective-permute-start | bytes 3145736 | tf_op jit(solution)/shard_map/ppermute | solution.py:11
  322.2 20.7 %copy-start.24 = (f32[1024,256]{1,0:T(8,128)}, f32[1024,256]{1,0:T(8,128)S(1)}, u32[]{:S(2)}) copy-start(f32[1024,256]{1,0:T(8,128)S(1)} %collective-permute-done.1) | copy-start | bytes 3145732
  326.0 118.1 %all-reduce.19.cloned.1.call-start = ((), (), s32[]{:S(2)}) async-start(), calls=%async_computation.5 | async-start | bytes 2097152 | tf_op jit(solution)/shard_map/psum | solution.py:47
  380.6 1.6 copy-start.9
  382.2 2.7 copy-start.4
  382.2 3.0 copy-start.25
  384.8 1.4 copy-start.17
  388.0 146.4 %all-reduce.21.cloned.1.call-start = ((), (), s32[]{:S(2)}) async-start(), calls=%async_computation.6 | async-start | bytes 2097152 | tf_op jit(solution)/shard_map/psum | solution.py:47
  444.1 4.2 copy-start.5
  450.0 26.0 %collective-permute-start.2 = (f32[1024,256]{1,0:T(8,128)}, f32[1024,256]{1,0:T(8,128)S(1)}, u32[]{:S(2)}, u32[]{:S(2)}) collective-permute-start(f32[1024,256]{1,0:T(8,128)} %fusion.47), channel_id=1, source_target_pairs={{0,2},{2,4},{4,6},{6,0},{1,3},{3,5},{5,7},{7,1},{8,10},{10,12},{12... | collective-permute-start | bytes 3145736 | tf_op jit(solution)/shard_map/ppermute | solution.py:11
  476.1 20.4 %copy-start.20 = (f32[1024,256]{1,0:T(8,128)}, f32[1024,256]{1,0:T(8,128)S(1)}, u32[]{:S(2)}) copy-start(f32[1024,256]{1,0:T(8,128)S(1)} %collective-permute-done.2) | copy-start | bytes 3145732
  479.8 118.0 %all-reduce.23.cloned.1.call-start = ((), (), s32[]{:S(2)}) async-start(), calls=%async_computation.7 | async-start | bytes 2097152 | tf_op jit(solution)/shard_map/psum | solution.py:47
  534.4 1.6 copy-start.8
  536.0 2.7 copy-start.6
  536.0 3.0 copy-start.21
  538.6 1.3 copy-start.12
  597.8 3.5 copy-start.7
  601.3 2.2 copy-start.13
  601.3 2.2 copy-start.15
  602.0 25.9 %collective-permute-start.3 = (f32[1024,256]{1,0:T(8,128)S(1)}, f32[1024,256]{1,0:T(8,128)S(1)}, u32[]{:S(2)}, u32[]{:S(2)}) collective-permute-start(f32[1024,256]{1,0:T(8,128)S(1)} %fusion.53), channel_id=1, source_target_pairs={{0,2},{2,4},{4,6},{6,0},{1,3},{3,5},{5,7},{7,1},{8,10},{10,12},{12... | collective-permute-start | bytes 3145736 | tf_op jit(solution)/shard_map/ppermute | solution.py:11
Sparse Core Ops, SparseCore 0:
  13.2 59.4 all-reduce.8
  80.1 56.4 all-reduce.10
  172.3 54.4 all-reduce.12
  234.3 55.9 all-reduce.14
  326.1 54.4 all-reduce.16
  388.1 55.9 all-reduce.18
  479.9 54.4 all-reduce.20
  541.8 55.9 all-reduce.22
where the time goes:
time: 639 us; the launch traced here: 636 us
  waiting for transfers between devices  285 us (45%)
  local copies, waits for them, and re-layouts  145 us (23%)
  blocking collectives  103 us (16%)
  matrix products  56.8 us (9%)
  between operations  33.9 us (5%)
    psum x8, waiting for transfers between devices, local(): scores, total_sq = lax.psum((partial_value, sq_part), ('ind', 'chip'))  194 us
    gather x8, local copies, waits for them, and re-layouts, posterior_step(): diag_part = jnp.diagonal(inverse).astype(jnp.float32)  122 us
    psum x8, blocking collectives, local(): scores, total_sq = lax.psum((partial_value, sq_part), ('ind', 'chip'))  103 us
    ppermute x4, waiting for transfers between devices, from_behind(): lax.ppermute(array, axis, [(i, (i + by) % peers) for i in range(peers)])  91 us
    dot_general x8, matrix products, posterior_step(): mean_part = jnp.dot(inverse, scaled, preferred_element_type=jnp.float32)  26.3 us
    dot_general x8, matrix products, local(): lax.dot_general(columns, current_low, (((0,), (0,)), ((), ())), preferred...  21.8 us
  transfers between devices with their start and end apart: 12, of which 12 were waited for; matrix products, arithmetic and copies ran while one was open for 22% of the time, Pallas kernels for 0%

commit v1 on v0

--- a/solution.py
+++ b/solution.py
@@ -44,7 +44,7 @@
             partial_value = lax.dot_general(
                 columns, current_low, (((0,), (0,)), ((), ())), preferred_element_type=jnp.float32
             )
-            scores, total_sq = lax.psum((partial_value, sq_part), ("ind", "chip"))
+            scores, total_sq = lax.psum(lax.psum((partial_value, sq_part), "chip"), "ind")
             change = posterior_step(inverse, scores, total_sq, noise_rows, count)
             stop_changes = lax.dynamic_update_slice_in_dim(
                 stop_changes, change, local_blk * block_len, 0

time: 639 us -> 826 us (1.29)
  waiting for transfers between devices: 285 us -> 486 us
  blocking collectives: 103 us -> 85.8 us
    psum x8 -> x16, waiting for transfers between devices: 194 us -> 393 us  [the longest x8 307 us: local(): lax.psum((partial_value, sq_part), 'chip')]
    psum x8 -> x16, blocking collectives: 103 us -> 85.8 us  [the longest x8 46.4 us: local(): lax.psum(lax.psum((partial_value, sq_part), 'chip'), 'ind')]
  transfers between devices with their start and end apart: 12 -> 20, of which waited for: 12 -> 19; matrix products, arithmetic and copies ran while one was open for 22% -> 17% of each run, Pallas kernels for 0% -> 0%
where the time goes in v1:
time: 826 us; the launch traced here: 822 us
  waiting for transfers between devices  486 us (59%)
  local copies, waits for them, and re-layouts  145 us (18%)
  blocking collectives  85.8 us (10%)
  matrix products  56.6 us (7%)
  between operations  35.5 us (4%)
    psum x8, waiting for transfers between devices, local(): lax.psum((partial_value, sq_part), 'chip')  307 us
    gather x8, local copies, waits for them, and re-layouts, posterior_step(): diag_part = jnp.diagonal(inverse).astype(jnp.float32)  122 us
    ppermute x4, waiting for transfers between devices, from_behind(): lax.ppermute(array, axis, [(i, (i + by) % peers) for i in range(peers)])  92.7 us
    psum x8, waiting for transfers between devices, local(): lax.psum(lax.psum((partial_value, sq_part), 'chip'), 'ind')  86.6 us
    psum x8, blocking collectives, local(): lax.psum(lax.psum((partial_value, sq_part), 'chip'), 'ind')  46.4 us
    psum x8, blocking collectives, local(): lax.psum((partial_value, sq_part), 'chip')  39.4 us
    dot_general x8, matrix products, posterior_step(): mean_part = jnp.dot(inverse, scaled, preferred_element_type=jnp.float32)  26.1 us
    dot_general x8, matrix products, local(): lax.dot_general(columns, current_low, (((0,), (0,)), ((), ())), preferred...  21.8 us
  transfers between devices with their start and end apart: 20, of which 19 were waited for; matrix products, arithmetic and copies ran while one was open for 17% of the time, Pallas kernels for 0%

profile of v1, /device:TPU:0, one launch (start us, length us, event | category | flops | bytes accessed | tf_op | source)
XLA Modules:
  0.0 821.9 jit_solution(7299351747010285231)
XLA Ops:
  29.0 27.2 %all-reduce.17.cloned.1.call-done = f32[1024,256]{1,0:T(8,128)} async-done(((f32[1024,256]{1,0:T(8,128)}), f32[1024,256]{1,0:T(8,128)}) %all-reduce.17.cloned.1.call-update) | async-done | bytes 1048592 | tf_op jit(solution)/shard_map/psum | solution.py:47
  56.2 11.6 %dynamic-slice_bitcast_fusion = (bf16[1024,1024]{1,0:T(8,128)(2,1)S(1)}, bf16[1024,1024]{1,0:T(8,128)(2,1)}, bf16[1024,1024]{1,0:T(8,128)(2,1)}, bf16[1024,1024]...) fusion(bf16[2,1024,1024]{2,1,0:T(8,128)(2,1)} %param.7, ...), kind=kLoop, calls=%fused_computation.9 | loop fusion | bytes 33554464 | tf_op jit(solution)/shard_map/jit(dynamic_index_in_dim)/squeeze | solution.py:39
  68.6 16.4 %gather_fusion = bf16[1024]{0:T(1024)(128)(2,1)S(1)} fusion(bf16[1024,1024]{1,0:T(8,128)(2,1)} %get-tuple-element.8, s32[1024]{0:T(1024)S(1)} %bitcast.81), kind=kCustom, calls=%fused_computation | custom fusion | bytes 12288 | tf_op jit(solution)/shard_map/jit(diagonal)/cond/branch_0_fun/gather | solution.py:18
  85.2 4.9 psum.226
  90.1 6.0 psum.227
  103.5 40.5 %all-reduce.21.cloned.1.call-done = f32[1024,256]{1,0:T(8,128)} async-done(((f32[1024,256]{1,0:T(8,128)}), f32[1024,256]{1,0:T(8,128)}) %all-reduce.21.cloned.1.call-update) | async-done | bytes 1048592 | tf_op jit(solution)/shard_map/psum | solution.py:47
  144.1 16.0 %gather_fusion.1 = bf16[1024]{0:T(1024)(128)(2,1)S(1)} fusion(bf16[1024,1024]{1,0:T(8,128)(2,1)} %get-tuple-element.7, s32[1024]{0:T(1024)S(1)} %bitcast.82), kind=kCustom, calls=%fused_computation.1 | custom fusion | bytes 12288 | tf_op jit(solution)/shard_map/jit(diagonal)/cond/branch_0_fun/gather | solution.py:18
  160.1 4.9 psum.230
  165.0 5.6 psum.231
  170.7 11.9 %all-reduce.23.cloned.1.call-done = f32[1024,256]{1,0:T(8,128)} async-done(((f32[1024,256]{1,0:T(8,128)}), f32[1024,256]{1,0:T(8,128)}) %all-reduce.23.cloned.1.call-update) | async-done | bytes 1048592 | tf_op jit(solution)/shard_map/psum | solution.py:47
  182.5 4.1 bitcast_dynamic-update-slice_fusion.6
  190.5 24.4 %collective-permute-done = f32[1024,256]{1,0:T(8,128)S(1)} collective-permute-done((f32[1024,256]{1,0:T(8,128)}, f32[1024,256]{1,0:T(8,128)S(1)}, u32[]{:S(2)}, u32[]{:S(2)}) %collective-permute-start) | collective-permute-done | bytes 1048608 | tf_op jit(solution)/shard_map/ppermute | solution.py:11
  218.7 39.0 %all-reduce.25.cloned.1.call-done = f32[1024,256]{1,0:T(8,128)} async-done(((f32[1024,256]{1,0:T(8,128)}), f32[1024,256]{1,0:T(8,128)}) %all-reduce.25.cloned.1.call-update) | async-done | bytes 1048592 | tf_op jit(solution)/shard_map/psum | solution.py:47
  258.5 16.1 %gather_fusion.2 = bf16[1024]{0:T(1024)(128)(2,1)S(1)} fusion(bf16[1024,1024]{1,0:T(8,128)(2,1)} %get-tuple-element.6, s32[1024]{0:T(1024)S(1)} %bitcast.83), kind=kCustom, calls=%fused_computation.2 | custom fusion | bytes 12288 | tf_op jit(solution)/shard_map/jit(diagonal)/cond/branch_0_fun/gather | solution.py:18
  274.8 4.9 psum.234
  279.7 5.8 psum.235
  285.5 10.8 %all-reduce.27.cloned.1.call-done = f32[1024,256]{1,0:T(8,128)} async-done(((f32[1024,256]{1,0:T(8,128)}), f32[1024,256]{1,0:T(8,128)}) %all-reduce.27.cloned.1.call-update) | async-done | bytes 1048592 | tf_op jit(solution)/shard_map/psum | solution.py:47
  303.6 40.7 %all-reduce.29.cloned.1.call-done = f32[1024,256]{1,0:T(8,128)} async-done(((f32[1024,256]{1,0:T(8,128)}), f32[1024,256]{1,0:T(8,128)}) %all-reduce.29.cloned.1.call-update) | async-done | bytes 1048592 | tf_op jit(solution)/shard_map/psum | solution.py:47
  344.4 16.2 %gather_fusion.3 = bf16[1024]{0:T(1024)(128)(2,1)S(1)} fusion(bf16[1024,1024]{1,0:T(8,128)(2,1)} %get-tuple-element.5, s32[1024]{0:T(1024)S(1)} %bitcast.84), kind=kCustom, calls=%fused_computation.3 | custom fusion | bytes 12288 | tf_op jit(solution)/shard_map/jit(diagonal)/cond/branch_0_fun/gather | solution.py:18
  360.5 4.9 psum.238
  365.5 5.6 psum.239
  371.1 11.9 %all-reduce.31.cloned.1.call-done = f32[1024,256]{1,0:T(8,128)} async-done(((f32[1024,256]{1,0:T(8,128)}), f32[1024,256]{1,0:T(8,128)}) %all-reduce.31.cloned.1.call-update) | async-done | bytes 1048592 | tf_op jit(solution)/shard_map/psum | solution.py:47
  383.0 4.1 bitcast_dynamic-update-slice_fusion.4
  391.0 24.4 %collective-permute-done.1 = f32[1024,256]{1,0:T(8,128)S(1)} collective-permute-done((f32[1024,256]{1,0:T(8,128)}, f32[1024,256]{1,0:T(8,128)S(1)}, u32[]{:S(2)}, u32[]{:S(2)}) %collective-permute-start.1) | collective-permute-done | bytes 1048608 | tf_op jit(solution)/shard_map/ppermute | solution.py:11
  419.2 39.0 %all-reduce.33.cloned.1.call-done = f32[1024,256]{1,0:T(8,128)} async-done(((f32[1024,256]{1,0:T(8,128)}), f32[1024,256]{1,0:T(8,128)}) %all-reduce.33.cloned.1.call-update) | async-done | bytes 1048592 | tf_op jit(solution)/shard_map/psum | solution.py:47
  458.9 16.2 %gather_fusion.4 = bf16[1024]{0:T(1024)(128)(2,1)S(1)} fusion(bf16[1024,1024]{1,0:T(8,128)(2,1)} %get-tuple-element.4, s32[1024]{0:T(1024)S(1)} %bitcast.85), kind=kCustom, calls=%fused_computation.4 | custom fusion | bytes 12288 | tf_op jit(solution)/shard_map/jit(diagonal)/cond/branch_0_fun/gather | solution.py:18
  475.4 4.9 psum.242
  480.3 5.6 psum.243
  485.9 10.8 %all-reduce.35.cloned.1.call-done = f32[1024,256]{1,0:T(8,128)} async-done(((f32[1024,256]{1,0:T(8,128)}), f32[1024,256]{1,0:T(8,128)}) %all-reduce.35.cloned.1.call-update) | async-done | bytes 1048592 | tf_op jit(solution)/shard_map/psum | solution.py:47
  504.1 40.7 %all-reduce.37.cloned.1.call-done = f32[1024,256]{1,0:T(8,128)} async-done(((f32[1024,256]{1,0:T(8,128)}), f32[1024,256]{1,0:T(8,128)}) %all-reduce.37.cloned.1.call-update) | async-done | bytes 1048592 | tf_op jit(solution)/shard_map/psum | solution.py:47
  544.9 15.8 %gather_fusion.5 = bf16[1024]{0:T(1024)(128)(2,1)S(1)} fusion(bf16[1024,1024]{1,0:T(8,128)(2,1)} %get-tuple-element.3, s32[1024]{0:T(1024)S(1)} %bitcast.86), kind=kCustom, calls=%fused_computation.5 | custom fusion | bytes 12288 | tf_op jit(solution)/shard_map/jit(diagonal)/cond/branch_0_fun/gather | solution.py:18
  560.7 4.9 psum.246
  565.7 5.9 psum.247
  571.5 11.8 %all-reduce.39.cloned.1.call-done = f32[1024,256]{1,0:T(8,128)} async-done(((f32[1024,256]{1,0:T(8,128)}), f32[1024,256]{1,0:T(8,128)}) %all-reduce.39.cloned.1.call-update) | async-done | bytes 1048592 | tf_op jit(solution)/shard_map/psum | solution.py:47
  583.4 4.2 bitcast_dynamic-update-slice_fusion.2
  591.5 24.4 %collective-permute-done.2 = f32[1024,256]{1,0:T(8,128)S(1)} collective-permute-done((f32[1024,256]{1,0:T(8,128)}, f32[1024,256]{1,0:T(8,128)S(1)}, u32[]{:S(2)}, u32[]{:S(2)}) %collective-permute-start.2) | collective-permute-done | bytes 1048608 | tf_op jit(solution)/shard_map/ppermute | solution.py:11
  619.6 39.0 %all-reduce.41.cloned.1.call-done = f32[1024,256]{1,0:T(8,128)} async-done(((f32[1024,256]{1,0:T(8,128)}), f32[1024,256]{1,0:T(8,128)}) %all-reduce.41.cloned.1.call-update) | async-done | bytes 1048592 | tf_op jit(solution)/shard_map/psum | solution.py:47
  659.4 16.0 %gather_fusion.6 = bf16[1024]{0:T(1024)(128)(2,1)S(1)} fusion(bf16[1024,1024]{1,0:T(8,128)(2,1)} %get-tuple-element.9, s32[1024]{0:T(1024)S(1)} %bitcast.87), kind=kCustom, calls=%fused_computation.6 | custom fusion | bytes 12288 | tf_op jit(solution)/shard_map/jit(diagonal)/cond/branch_0_fun/gather | solution.py:18
  675.5 4.9 psum.250
  680.5 5.6 psum.251
  686.1 11.1 %all-reduce.43.cloned.1.call-done = f32[1024,256]{1,0:T(8,128)} async-done(((f32[1024,256]{1,0:T(8,128)}), f32[1024,256]{1,0:T(8,128)}) %all-reduce.43.cloned.1.call-update) | async-done | bytes 1048592 | tf_op jit(solution)/shard_map/psum | solution.py:47
  704.5 40.7 %all-reduce.45.cloned.1.call-done = f32[1024,256]{1,0:T(8,128)} async-done(((f32[1024,256]{1,0:T(8,128)}), f32[1024,256]{1,0:T(8,128)}) %all-reduce.45.cloned.1.call-update) | async-done | bytes 1048592 | tf_op jit(solution)/shard_map/psum | solution.py:47
  745.2 9.1 %gather_fusion.7 = bf16[1024]{0:T(1024)(128)(2,1)S(1)} fusion(bf16[1024,1024]{1,0:T(8,128)(2,1)S(1)} %get-tuple-element.2, s32[1024]{0:T(1024)S(1)} %bitcast.88), kind=kCustom, calls=%fused_computation.7 | custom fusion | bytes 12288 | tf_op jit(solution)/shard_map/jit(diagonal)/cond/branch_0_fun/gather | solution.py:18
  754.3 4.9 psum.254
  759.3 6.1 psum.255
  765.4 18.3 %all-reduce.47.cloned.1.call-done = f32[1024,256]{1,0:T(8,128)} async-done(((f32[1024,256]{1,0:T(8,128)}), f32[1024,256]{1,0:T(8,128)}) %all-reduce.47.cloned.1.call-update) | async-done | bytes 1048592 | tf_op jit(solution)/shard_map/psum | solution.py:47
  789.5 5.3 pad_maximum_fusion
  794.8 19.5 %collective-permute-done.3 = f32[1024,256]{1,0:T(8,128)S(1)} collective-permute-done((f32[1024,256]{1,0:T(8,128)S(1)}, f32[1024,256]{1,0:T(8,128)S(1)}, u32[]{:S(2)}, u32[]{:S(2)}) %collective-permute-start.3) | collective-permute-done | bytes 1048608 | tf_op jit(solution)/shard_map/ppermute | solution.py:11
  (137 shorter events, 63.2 us)
Async XLA Ops:
  7.2 49.0 %all-reduce.17.cloned.1.call-start = ((), (), s32[]{:S(2)}) async-start(), calls=%async_computation | async-start | bytes 2097152 | tf_op jit(solution)/shard_map/psum | solution.py:47
  13.1 83.1 %all-reduce.19.cloned.1.call-start = ((), (), s32[]{:S(2)}) async-start(), calls=%async_computation.1 | async-start | bytes 2097152 | tf_op jit(solution)/shard_map/psum | solution.py:47
  56.1 87.9 %all-reduce.21.cloned.1.call-start = ((), (), s32[]{:S(2)}) async-start(), calls=%async_computation.2 | async-start | bytes 2097152 | tf_op jit(solution)/shard_map/psum | solution.py:47
  67.8 17.2 %copy-start.18 = (f32[1024,256]{1,0:T(8,128)S(1)}, f32[1024,256]{1,0:T(8,128)}, u32[]{:S(2)}) copy-start(f32[1024,256]{1,0:T(8,128)} %param.6) | copy-start | bytes 3145732
  96.2 1.6 copy-start.11
  97.8 2.7 copy-start
  97.8 3.0 copy-start.19
  100.3 1.3 copy-start.14
  103.4 79.1 %all-reduce.23.cloned.1.call-start = ((), (), s32[]{:S(2)}) async-start(), calls=%async_computation.3 | async-start | bytes 2097152 | tf_op jit(solution)/shard_map/psum | solution.py:47
  144.0 113.7 %all-reduce.25.cloned.1.call-start = ((), (), s32[]{:S(2)}) async-start(), calls=%async_computation.4 | async-start | bytes 2097152 | tf_op jit(solution)/shard_map/psum | solution.py:47
  182.5 4.1 copy-start.1
  188.3 26.6 %collective-permute-start = (f32[1024,256]{1,0:T(8,128)}, f32[1024,256]{1,0:T(8,128)S(1)}, u32[]{:S(2)}, u32[]{:S(2)}) collective-permute-start(f32[1024,256]{1,0:T(8,128)} %fusion.35), channel_id=1, source_target_pairs={{0,2},{2,4},{4,6},{6,0},{1,3},{3,5},{5,7},{7,1},{8,10},{10,12},{12... | collective-permute-start | bytes 3145736 | tf_op jit(solution)/shard_map/ppermute | solution.py:11
  214.9 59.7 %copy-start.22 = (f32[1024,256]{1,0:T(8,128)}, f32[1024,256]{1,0:T(8,128)S(1)}, u32[]{:S(2)}) copy-start(f32[1024,256]{1,0:T(8,128)S(1)} %collective-permute-done) | copy-start | bytes 3145732
  218.7 77.6 %all-reduce.27.cloned.1.call-start = ((), (), s32[]{:S(2)}) async-start(), calls=%async_computation.5 | async-start | bytes 2097152 | tf_op jit(solution)/shard_map/psum | solution.py:47
  257.8 86.5 %all-reduce.29.cloned.1.call-start = ((), (), s32[]{:S(2)}) async-start(), calls=%async_computation.6 | async-start | bytes 2097152 | tf_op jit(solution)/shard_map/psum | solution.py:47
  296.3 1.6 copy-start.10
  297.9 2.7 copy-start.2
  297.9 3.0 copy-start.23
  300.4 1.3 copy-start.16
  303.5 79.4 %all-reduce.31.cloned.1.call-start = ((), (), s32[]{:S(2)}) async-start(), calls=%async_computation.7 | async-start | bytes 2097152 | tf_op jit(solution)/shard_map/psum | solution.py:47
  344.3 113.9 %all-reduce.33.cloned.1.call-start = ((), (), s32[]{:S(2)}) async-start(), calls=%async_computation.8 | async-start | bytes 2097152 | tf_op jit(solution)/shard_map/psum | solution.py:47
  383.0 4.2 copy-start.3
  388.8 26.6 %collective-permute-start.1 = (f32[1024,256]{1,0:T(8,128)}, f32[1024,256]{1,0:T(8,128)S(1)}, u32[]{:S(2)}, u32[]{:S(2)}) collective-permute-start(f32[1024,256]{1,0:T(8,128)} %fusion.41), channel_id=1, source_target_pairs={{0,2},{2,4},{4,6},{6,0},{1,3},{3,5},{5,7},{7,1},{8,10},{10,12},{12... | collective-permute-start | bytes 3145736 | tf_op jit(solution)/shard_map/ppermute | solution.py:11
  415.4 59.8 %copy-start.24 = (f32[1024,256]{1,0:T(8,128)}, f32[1024,256]{1,0:T(8,128)S(1)}, u32[]{:S(2)}) copy-start(f32[1024,256]{1,0:T(8,128)S(1)} %collective-permute-done.1) | copy-start | bytes 3145732
  419.2 77.6 %all-reduce.35.cloned.1.call-start = ((), (), s32[]{:S(2)}) async-start(), calls=%async_computation.9 | async-start | bytes 2097152 | tf_op jit(solution)/shard_map/psum | solution.py:47
  458.3 86.6 %all-reduce.37.cloned.1.call-start = ((), (), s32[]{:S(2)}) async-start(), calls=%async_computation.10 | async-start | bytes 2097152 | tf_op jit(solution)/shard_map/psum | solution.py:47
  496.8 1.6 copy-start.9
  498.4 2.7 copy-start.4
  498.4 3.0 copy-start.25
  500.9 1.4 copy-start.17
  504.1 79.3 %all-reduce.39.cloned.1.call-start = ((), (), s32[]{:S(2)}) async-start(), calls=%async_computation.11 | async-start | bytes 2097152 | tf_op jit(solution)/shard_map/psum | solution.py:47
  544.9 113.8 %all-reduce.41.cloned.1.call-start = ((), (), s32[]{:S(2)}) async-start(), calls=%async_computation.12 | async-start | bytes 2097152 | tf_op jit(solution)/shard_map/psum | solution.py:47
  583.4 4.2 copy-start.5
  589.3 26.6 %collective-permute-start.2 = (f32[1024,256]{1,0:T(8,128)}, f32[1024,256]{1,0:T(8,128)S(1)}, u32[]{:S(2)}, u32[]{:S(2)}) collective-permute-start(f32[1024,256]{1,0:T(8,128)} %fusion.47), channel_id=1, source_target_pairs={{0,2},{2,4},{4,6},{6,0},{1,3},{3,5},{5,7},{7,1},{8,10},{10,12},{12... | collective-permute-start | bytes 3145736 | tf_op jit(solution)/shard_map/ppermute | solution.py:11
  615.8 59.5 %copy-start.20 = (f32[1024,256]{1,0:T(8,128)}, f32[1024,256]{1,0:T(8,128)S(1)}, u32[]{:S(2)}) copy-start(f32[1024,256]{1,0:T(8,128)S(1)} %collective-permute-done.2) | copy-start | bytes 3145732
  619.6 77.6 %all-reduce.43.cloned.1.call-start = ((), (), s32[]{:S(2)}) async-start(), calls=%async_computation.13 | async-start | bytes 2097152 | tf_op jit(solution)/shard_map/psum | solution.py:47
  658.7 86.5 %all-reduce.45.cloned.1.call-start = ((), (), s32[]{:S(2)}) async-start(), calls=%async_computation.14 | async-start | bytes 2097152 | tf_op jit(solution)/shard_map/psum | solution.py:47
  697.2 1.6 copy-start.8
  698.8 2.7 copy-start.6
  698.8 3.0 copy-start.21
  701.3 1.3 copy-start.12
  704.4 79.3 %all-reduce.47.cloned.1.call-start = ((), (), s32[]{:S(2)}) async-start(), calls=%async_computation.15 | async-start | bytes 2097152 | tf_op jit(solution)/shard_map/psum | solution.py:47
  783.7 3.5 copy-start.7
  787.2 2.3 copy-start.13
  787.2 2.3 copy-start.15
  788.0 26.4 %collective-permute-start.3 = (f32[1024,256]{1,0:T(8,128)S(1)}, f32[1024,256]{1,0:T(8,128)S(1)}, u32[]{:S(2)}, u32[]{:S(2)}) collective-permute-start(f32[1024,256]{1,0:T(8,128)S(1)} %fusion.53), channel_id=1, source_target_pairs={{0,2},{2,4},{4,6},{6,0},{1,3},{3,5},{5,7},{7,1},{8,10},{10,12},{12... | collective-permute-start | bytes 3145736 | tf_op jit(solution)/shard_map/ppermute | solution.py:11
Sparse Core Ops, SparseCore 0:
  13.2 42.8 all-reduce.16
  58.5 36.3 all-reduce.18
  103.5 40.4 all-reduce.20
  146.2 36.2 all-reduce.22
  218.8 38.9 all-reduce.24
  260.0 36.2 all-reduce.26
  303.7 40.5 all-reduce.28
  346.6 36.2 all-reduce.30
  419.3 38.9 all-reduce.32
  460.5 36.2 all-reduce.34
  504.2 40.5 all-reduce.36
  547.0 36.2 all-reduce.38
  619.7 38.9 all-reduce.40
  660.9 36.2 all-reduce.42
  704.6 40.5 all-reduce.44
  747.4 36.2 all-reduce.46
